TPU v7x, 512 devices: a whole 4x8x8 slice. The times are simulated.
512 devices in a mesh: head: 16 (over y, z_hi), seq: 32 (over x, z_lo, core).
Axes of the slice: x: 4, y: 8, z: 8 (z_hi: 2, z_lo: 4; z = z_hi * 4 + z_lo), core: 2. Of those that a mesh axis runs over, the one named last changes fastest.
Arguments:
- queries: bfloat16 [1, 32768, 8192], P(None, 'seq', 'head'), may hold values from -6 to 6
- keys: bfloat16 [1, 32768, 8192], P(None, 'seq', 'head'), may hold values from -6 to 6
- values: bfloat16 [1, 32768, 8192], P(None, 'seq', 'head'), may hold values from -60 to 60
- decay_rate: float32 [64], P('head'), may hold values from 1.5258789e-07 to 0.03
- norm_gain: float32 [8192], P('head'), may hold values from 0.25 to 1.75
- offsets: int32 [1], replicated, may hold values from 0 to 31
Outputs:
- normed: bfloat16 [1, 32768, 8192], P(None, 'seq', 'head')
All inputs are finite; a program needn't handle non-finite values.
Results may differ from a plain program's by a relative error of at most 0.0044.
Values sent between devices are 32-bit elements; how exact they have to be, the bound alone decides.
No kernel may reach another device: no remote copies, remote signals or barrier semaphores. Data moves between devices by JAX's collectives and lax.ppermute only.
A program may use at most 64 MiB of HBM per device.

v0:
```python
import jax
import jax.numpy as jnp
from jax import lax
from jax.sharding import PartitionSpec as P

epsilon = 1e-05


def from_behind(shard, axis, by):
    count = lax.axis_size(axis)
    return lax.ppermute(shard, axis, [(i, (i + by) % count) for i in range(count)])


def body(queries, keys, values, decay_rate, norm_gain, offsets):
    seq_count, block_len, columns = queries.shape
    heads_dev = decay_rate.shape[0]
    head_size = columns // heads_dev
    shaped = (seq_count, block_len, heads_dev, head_size)
    query_heads = queries.reshape(shaped)
    key_heads = keys.reshape(shaped)
    value_heads = values.reshape(shaped)
    places = jnp.arange(block_len).astype(jnp.float32)
    distance = places[:, None] - places[None, :]
    within = (
        jnp.exp(-decay_rate[:, None, None] * jnp.maximum(distance, 0.0)[None])
        * (distance >= 0.0).astype(jnp.float32)[None]
    )
    scores = jnp.einsum(
        "sihd,sjhd->shij", query_heads, key_heads, preferred_element_type=jnp.float32
    )
    weights = (scores * within[None]).astype(jnp.bfloat16)
    inner_part = jnp.einsum(
        "shij,sjhd->sihd", weights, value_heads, preferred_element_type=jnp.float32
    )
    key_scale = jnp.exp(-decay_rate[None, :] * (block_len - 1.0 - places[:, None]))
    decayed_keys = (key_heads.astype(jnp.float32) * key_scale[None, :, :, None]).astype(
        jnp.bfloat16
    )
    local_state = jnp.einsum(
        "sjhd,sjhe->shde", decayed_keys, value_heads, preferred_element_type=jnp.float32
    )
    group_decay = jnp.exp(-decay_rate * block_len)[None, :, None, None]
    cycle_size = lax.axis_size("seq")
    loop_place = lax.axis_index("seq")
    group_index = jnp.mod(loop_place - offsets, cycle_size)

    def follows(stride):
        return (group_index >= stride).astype(jnp.float32)[:, None, None, None]

    def advance(turn_index, incoming):
        outgoing = local_state + group_decay * incoming
        return follows(1) * from_behind(outgoing, "seq", 1)

    incoming = lax.fori_loop(0, cycle_size - 1, advance, jnp.zeros_like(local_state))
    query_scale = jnp.exp(-decay_rate[None, :] * (places[:, None] + 1.0))
    scaled_queries = query_heads.astype(jnp.float32) * query_scale[None, :, :, None]
    carried_part = jnp.einsum(
        "sihd,shde->sihe", scaled_queries, incoming, precision=lax.Precision.HIGHEST
    )
    attended = (inner_part + carried_part).reshape(seq_count, block_len, columns)
    squares = jnp.sum(attended * attended, axis=-1)
    sum_squares = lax.psum(squares, "head")
    features_all = columns * lax.axis_size("head")
    inv_rms = lax.rsqrt(sum_squares / features_all + epsilon)
    return (attended * inv_rms[..., None] * norm_gain).astype(jnp.bfloat16)


def solution(mesh):
    in_specs = (
        P(None, "seq", "head"),
        P(None, "seq", "head"),
        P(None, "seq", "head"),
        P("head"),
        P("head"),
        P(),
    )
    out_specs = P(None, "seq", "head")
    return jax.shard_map(body, mesh=mesh, in_specs=in_specs, out_specs=out_specs, check_vma=False)
```

profile of v0, /device:TPU:8, one launch (start us, length us, event | category | flops | bytes accessed | tf_op | source)
XLA Modules:
  0.0 450.2 jit_solution(8367281808237662304)
XLA Ops:
  7.3 365.9 %while.13 = (s32[]{:T(128)}, f32[1,4,128,128]{3,2,1,0:T(8,128)S(1)}, pred[1]{0:T(512)(128)(4,1)}, f32[1,4,1,1]{1,3,2,0:T(1,128)S(1)}, f32[1,4,128,128]{3,2,1,0:T(8,128)S(1)}, /*index=5*/s32[]{:T(128)}, s32[]{:T(128)}) while((s32[]{:T(128)}, f32[1,4,128,128]{3,2,1,0:T(8,128)S(1)}, pred[1]{0:T(512)(128)(4,1)}, ...), condition=%wide.region_1.2_spmd.clone, body=%wide.region_0.1_spmd.clone.sunk | while | flops 262148 | bytes 2359448 | solution.py:54
  9.3 11.6 %collective-permute-done = f32[1,4,128,128]{3,2,1,0:T(8,128)S(1)} collective-permute-done((f32[1,4,128,128]{3,2,1,0:T(8,128)S(1)}, f32[1,4,128,128]{3,2,1,0:T(8,128)S(1)}, u32[]{:S(2)}, u32[]{:S(2)}) %collective-permute-start) | collective-permute-done | bytes 262176 | tf_op jit(solution)/shard_map/while/body/eval_jaxpr/ppermute | solution.py:11
  23.0 9.7 %collective-permute-done = f32[1,4,128,128]{3,2,1,0:T(8,128)S(1)} collective-permute-done((f32[1,4,128,128]{3,2,1,0:T(8,128)S(1)}, f32[1,4,128,128]{3,2,1,0:T(8,128)S(1)}, u32[]{:S(2)}, u32[]{:S(2)}) %collective-permute-start) | collective-permute-done | bytes 262176 | tf_op jit(solution)/shard_map/while/body/eval_jaxpr/ppermute | solution.py:11
  34.8 9.7 %collective-permute-done = f32[1,4,128,128]{3,2,1,0:T(8,128)S(1)} collective-permute-done((f32[1,4,128,128]{3,2,1,0:T(8,128)S(1)}, f32[1,4,128,128]{3,2,1,0:T(8,128)S(1)}, u32[]{:S(2)}, u32[]{:S(2)}) %collective-permute-start) | collective-permute-done | bytes 262176 | tf_op jit(solution)/shard_map/while/body/eval_jaxpr/ppermute | solution.py:11
  46.5 9.7 %collective-permute-done = f32[1,4,128,128]{3,2,1,0:T(8,128)S(1)} collective-permute-done((f32[1,4,128,128]{3,2,1,0:T(8,128)S(1)}, f32[1,4,128,128]{3,2,1,0:T(8,128)S(1)}, u32[]{:S(2)}, u32[]{:S(2)}) %collective-permute-start) | collective-permute-done | bytes 262176 | tf_op jit(solution)/shard_map/while/body/eval_jaxpr/ppermute | solution.py:11
  58.2 9.7 %collective-permute-done = f32[1,4,128,128]{3,2,1,0:T(8,128)S(1)} collective-permute-done((f32[1,4,128,128]{3,2,1,0:T(8,128)S(1)}, f32[1,4,128,128]{3,2,1,0:T(8,128)S(1)}, u32[]{:S(2)}, u32[]{:S(2)}) %collective-permute-start) | collective-permute-done | bytes 262176 | tf_op jit(solution)/shard_map/while/body/eval_jaxpr/ppermute | solution.py:11
  70.0 9.7 %collective-permute-done = f32[1,4,128,128]{3,2,1,0:T(8,128)S(1)} collective-permute-done((f32[1,4,128,128]{3,2,1,0:T(8,128)S(1)}, f32[1,4,128,128]{3,2,1,0:T(8,128)S(1)}, u32[]{:S(2)}, u32[]{:S(2)}) %collective-permute-start) | collective-permute-done | bytes 262176 | tf_op jit(solution)/shard_map/while/body/eval_jaxpr/ppermute | solution.py:11
  81.7 9.7 %collective-permute-done = f32[1,4,128,128]{3,2,1,0:T(8,128)S(1)} collective-permute-done((f32[1,4,128,128]{3,2,1,0:T(8,128)S(1)}, f32[1,4,128,128]{3,2,1,0:T(8,128)S(1)}, u32[]{:S(2)}, u32[]{:S(2)}) %collective-permute-start) | collective-permute-done | bytes 262176 | tf_op jit(solution)/shard_map/while/body/eval_jaxpr/ppermute | solution.py:11
  93.4 9.7 %collective-permute-done = f32[1,4,128,128]{3,2,1,0:T(8,128)S(1)} collective-permute-done((f32[1,4,128,128]{3,2,1,0:T(8,128)S(1)}, f32[1,4,128,128]{3,2,1,0:T(8,128)S(1)}, u32[]{:S(2)}, u32[]{:S(2)}) %collective-permute-start) | collective-permute-done | bytes 262176 | tf_op jit(solution)/shard_map/while/body/eval_jaxpr/ppermute | solution.py:11
  105.2 9.7 %collective-permute-done = f32[1,4,128,128]{3,2,1,0:T(8,128)S(1)} collective-permute-done((f32[1,4,128,128]{3,2,1,0:T(8,128)S(1)}, f32[1,4,128,128]{3,2,1,0:T(8,128)S(1)}, u32[]{:S(2)}, u32[]{:S(2)}) %collective-permute-start) | collective-permute-done | bytes 262176 | tf_op jit(solution)/shard_map/while/body/eval_jaxpr/ppermute | solution.py:11
  116.9 9.7 %collective-permute-done = f32[1,4,128,128]{3,2,1,0:T(8,128)S(1)} collective-permute-done((f32[1,4,128,128]{3,2,1,0:T(8,128)S(1)}, f32[1,4,128,128]{3,2,1,0:T(8,128)S(1)}, u32[]{:S(2)}, u32[]{:S(2)}) %collective-permute-start) | collective-permute-done | bytes 262176 | tf_op jit(solution)/shard_map/while/body/eval_jaxpr/ppermute | solution.py:11
  128.6 9.7 %collective-permute-done = f32[1,4,128,128]{3,2,1,0:T(8,128)S(1)} collective-permute-done((f32[1,4,128,128]{3,2,1,0:T(8,128)S(1)}, f32[1,4,128,128]{3,2,1,0:T(8,128)S(1)}, u32[]{:S(2)}, u32[]{:S(2)}) %collective-permute-start) | collective-permute-done | bytes 262176 | tf_op jit(solution)/shard_map/while/body/eval_jaxpr/ppermute | solution.py:11
  140.4 9.7 %collective-permute-done = f32[1,4,128,128]{3,2,1,0:T(8,128)S(1)} collective-permute-done((f32[1,4,128,128]{3,2,1,0:T(8,128)S(1)}, f32[1,4,128,128]{3,2,1,0:T(8,128)S(1)}, u32[]{:S(2)}, u32[]{:S(2)}) %collective-permute-start) | collective-permute-done | bytes 262176 | tf_op jit(solution)/shard_map/while/body/eval_jaxpr/ppermute | solution.py:11
  152.1 9.7 %collective-permute-done = f32[1,4,128,128]{3,2,1,0:T(8,128)S(1)} collective-permute-done((f32[1,4,128,128]{3,2,1,0:T(8,128)S(1)}, f32[1,4,128,128]{3,2,1,0:T(8,128)S(1)}, u32[]{:S(2)}, u32[]{:S(2)}) %collective-permute-start) | collective-permute-done | bytes 262176 | tf_op jit(solution)/shard_map/while/body/eval_jaxpr/ppermute | solution.py:11
  163.9 9.7 %collective-permute-done = f32[1,4,128,128]{3,2,1,0:T(8,128)S(1)} collective-permute-done((f32[1,4,128,128]{3,2,1,0:T(8,128)S(1)}, f32[1,4,128,128]{3,2,1,0:T(8,128)S(1)}, u32[]{:S(2)}, u32[]{:S(2)}) %collective-permute-start) | collective-permute-done | bytes 262176 | tf_op jit(solution)/shard_map/while/body/eval_jaxpr/ppermute | solution.py:11
  175.6 9.7 %collective-permute-done = f32[1,4,128,128]{3,2,1,0:T(8,128)S(1)} collective-permute-done((f32[1,4,128,128]{3,2,1,0:T(8,128)S(1)}, f32[1,4,128,128]{3,2,1,0:T(8,128)S(1)}, u32[]{:S(2)}, u32[]{:S(2)}) %collective-permute-start) | collective-permute-done | bytes 262176 | tf_op jit(solution)/shard_map/while/body/eval_jaxpr/ppermute | solution.py:11
  187.3 9.7 %collective-permute-done = f32[1,4,128,128]{3,2,1,0:T(8,128)S(1)} collective-permute-done((f32[1,4,128,128]{3,2,1,0:T(8,128)S(1)}, f32[1,4,128,128]{3,2,1,0:T(8,128)S(1)}, u32[]{:S(2)}, u32[]{:S(2)}) %collective-permute-start) | collective-permute-done | bytes 262176 | tf_op jit(solution)/shard_map/while/body/eval_jaxpr/ppermute | solution.py:11
  199.1 9.7 %collective-permute-done = f32[1,4,128,128]{3,2,1,0:T(8,128)S(1)} collective-permute-done((f32[1,4,128,128]{3,2,1,0:T(8,128)S(1)}, f32[1,4,128,128]{3,2,1,0:T(8,128)S(1)}, u32[]{:S(2)}, u32[]{:S(2)}) %collective-permute-start) | collective-permute-done | bytes 262176 | tf_op jit(solution)/shard_map/while/body/eval_jaxpr/ppermute | solution.py:11
  210.8 9.7 %collective-permute-done = f32[1,4,128,128]{3,2,1,0:T(8,128)S(1)} collective-permute-done((f32[1,4,128,128]{3,2,1,0:T(8,128)S(1)}, f32[1,4,128,128]{3,2,1,0:T(8,128)S(1)}, u32[]{:S(2)}, u32[]{:S(2)}) %collective-permute-start) | collective-permute-done | bytes 262176 | tf_op jit(solution)/shard_map/while/body/eval_jaxpr/ppermute | solution.py:11
  222.5 9.7 %collective-permute-done = f32[1,4,128,128]{3,2,1,0:T(8,128)S(1)} collective-permute-done((f32[1,4,128,128]{3,2,1,0:T(8,128)S(1)}, f32[1,4,128,128]{3,2,1,0:T(8,128)S(1)}, u32[]{:S(2)}, u32[]{:S(2)}) %collective-permute-start) | collective-permute-done | bytes 262176 | tf_op jit(solution)/shard_map/while/body/eval_jaxpr/ppermute | solution.py:11
  234.3 9.7 %collective-permute-done = f32[1,4,128,128]{3,2,1,0:T(8,128)S(1)} collective-permute-done((f32[1,4,128,128]{3,2,1,0:T(8,128)S(1)}, f32[1,4,128,128]{3,2,1,0:T(8,128)S(1)}, u32[]{:S(2)}, u32[]{:S(2)}) %collective-permute-start) | collective-permute-done | bytes 262176 | tf_op jit(solution)/shard_map/while/body/eval_jaxpr/ppermute | solution.py:11
  246.0 9.7 %collective-permute-done = f32[1,4,128,128]{3,2,1,0:T(8,128)S(1)} collective-permute-done((f32[1,4,128,128]{3,2,1,0:T(8,128)S(1)}, f32[1,4,128,128]{3,2,1,0:T(8,128)S(1)}, u32[]{:S(2)}, u32[]{:S(2)}) %collective-permute-start) | collective-permute-done | bytes 262176 | tf_op jit(solution)/shard_map/while/body/eval_jaxpr/ppermute | solution.py:11
  257.7 9.7 %collective-permute-done = f32[1,4,128,128]{3,2,1,0:T(8,128)S(1)} collective-permute-done((f32[1,4,128,128]{3,2,1,0:T(8,128)S(1)}, f32[1,4,128,128]{3,2,1,0:T(8,128)S(1)}, u32[]{:S(2)}, u32[]{:S(2)}) %collective-permute-start) | collective-permute-done | bytes 262176 | tf_op jit(solution)/shard_map/while/body/eval_jaxpr/ppermute | solution.py:11
  269.5 9.7 %collective-permute-done = f32[1,4,128,128]{3,2,1,0:T(8,128)S(1)} collective-permute-done((f32[1,4,128,128]{3,2,1,0:T(8,128)S(1)}, f32[1,4,128,128]{3,2,1,0:T(8,128)S(1)}, u32[]{:S(2)}, u32[]{:S(2)}) %collective-permute-start) | collective-permute-done | bytes 262176 | tf_op jit(solution)/shard_map/while/body/eval_jaxpr/ppermute | solution.py:11
  281.2 9.7 %collective-permute-done = f32[1,4,128,128]{3,2,1,0:T(8,128)S(1)} collective-permute-done((f32[1,4,128,128]{3,2,1,0:T(8,128)S(1)}, f32[1,4,128,128]{3,2,1,0:T(8,128)S(1)}, u32[]{:S(2)}, u32[]{:S(2)}) %collective-permute-start) | collective-permute-done | bytes 262176 | tf_op jit(solution)/shard_map/while/body/eval_jaxpr/ppermute | solution.py:11
  292.9 9.7 %collective-permute-done = f32[1,4,128,128]{3,2,1,0:T(8,128)S(1)} collective-permute-done((f32[1,4,128,128]{3,2,1,0:T(8,128)S(1)}, f32[1,4,128,128]{3,2,1,0:T(8,128)S(1)}, u32[]{:S(2)}, u32[]{:S(2)}) %collective-permute-start) | collective-permute-done | bytes 262176 | tf_op jit(solution)/shard_map/while/body/eval_jaxpr/ppermute | solution.py:11
  304.7 9.7 %collective-permute-done = f32[1,4,128,128]{3,2,1,0:T(8,128)S(1)} collective-permute-done((f32[1,4,128,128]{3,2,1,0:T(8,128)S(1)}, f32[1,4,128,128]{3,2,1,0:T(8,128)S(1)}, u32[]{:S(2)}, u32[]{:S(2)}) %collective-permute-start) | collective-permute-done | bytes 262176 | tf_op jit(solution)/shard_map/while/body/eval_jaxpr/ppermute | solution.py:11
  316.4 9.7 %collective-permute-done = f32[1,4,128,128]{3,2,1,0:T(8,128)S(1)} collective-permute-done((f32[1,4,128,128]{3,2,1,0:T(8,128)S(1)}, f32[1,4,128,128]{3,2,1,0:T(8,128)S(1)}, u32[]{:S(2)}, u32[]{:S(2)}) %collective-permute-start) | collective-permute-done | bytes 262176 | tf_op jit(solution)/shard_map/while/body/eval_jaxpr/ppermute | solution.py:11
  328.1 9.7 %collective-permute-done = f32[1,4,128,128]{3,2,1,0:T(8,128)S(1)} collective-permute-done((f32[1,4,128,128]{3,2,1,0:T(8,128)S(1)}, f32[1,4,128,128]{3,2,1,0:T(8,128)S(1)}, u32[]{:S(2)}, u32[]{:S(2)}) %collective-permute-start) | collective-permute-done | bytes 262176 | tf_op jit(solution)/shard_map/while/body/eval_jaxpr/ppermute | solution.py:11
  339.9 9.7 %collective-permute-done = f32[1,4,128,128]{3,2,1,0:T(8,128)S(1)} collective-permute-done((f32[1,4,128,128]{3,2,1,0:T(8,128)S(1)}, f32[1,4,128,128]{3,2,1,0:T(8,128)S(1)}, u32[]{:S(2)}, u32[]{:S(2)}) %collective-permute-start) | collective-permute-done | bytes 262176 | tf_op jit(solution)/shard_map/while/body/eval_jaxpr/ppermute | solution.py:11
  363.4 9.8 %collective-permute-done = f32[1,4,128,128]{3,2,1,0:T(8,128)S(1)} collective-permute-done((f32[1,4,128,128]{3,2,1,0:T(8,128)S(1)}, f32[1,4,128,128]{3,2,1,0:T(8,128)S(1)}, u32[]{:S(2)}, u32[]{:S(2)}) %collective-permute-start) | collective-permute-done | bytes 262176 | tf_op jit(solution)/shard_map/while/body/eval_jaxpr/ppermute | solution.py:11
  391.5 54.0 %psum.7 = f32[1,1024]{1,0:T(1,128)S(1)} all-reduce(f32[1,1024]{1,0:T(1,128)S(1)} %bitcast.33), channel_id=1, replica_groups=mesh['head'=16,'seq'=32] {'head'}, use_global_device_ids=true, to_apply=%region_3.4 | all-reduce | flops 1024 | bytes 8192 | tf_op jit(solution)/shard_map/psum | solution.py:62
  (116 shorter events, 102.2 us)
Async XLA Ops:
  7.4 13.6 %collective-permute-start = (f32[1,4,128,128]{3,2,1,0:T(8,128)S(1)}, f32[1,4,128,128]{3,2,1,0:T(8,128)S(1)}, u32[]{:S(2)}, u32[]{:S(2)}) collective-permute-start(f32[1,4,128,128]{3,2,1,0:T(8,128)S(1)} %fusion.21), channel_id=1, source_target_pairs={{0,1},{1,2},{2,3},{3,4},{4,5},{5,6},{6,7},{7,8},{8,9},{9,10},{10,1... | collective-permute-start | bytes 786440 | tf_op jit(solution)/shard_map/while/body/eval_jaxpr/ppermute | solution.py:11
  21.1 11.6 %collective-permute-start = (f32[1,4,128,128]{3,2,1,0:T(8,128)S(1)}, f32[1,4,128,128]{3,2,1,0:T(8,128)S(1)}, u32[]{:S(2)}, u32[]{:S(2)}) collective-permute-start(f32[1,4,128,128]{3,2,1,0:T(8,128)S(1)} %fusion.21), channel_id=1, source_target_pairs={{0,1},{1,2},{2,3},{3,4},{4,5},{5,6},{6,7},{7,8},{8,9},{9,10},{10,1... | collective-permute-start | bytes 786440 | tf_op jit(solution)/shard_map/while/body/eval_jaxpr/ppermute | solution.py:11
  32.8 11.6 %collective-permute-start = (f32[1,4,128,128]{3,2,1,0:T(8,128)S(1)}, f32[1,4,128,128]{3,2,1,0:T(8,128)S(1)}, u32[]{:S(2)}, u32[]{:S(2)}) collective-permute-start(f32[1,4,128,128]{3,2,1,0:T(8,128)S(1)} %fusion.21), channel_id=1, source_target_pairs={{0,1},{1,2},{2,3},{3,4},{4,5},{5,6},{6,7},{7,8},{8,9},{9,10},{10,1... | collective-permute-start | bytes 786440 | tf_op jit(solution)/shard_map/while/body/eval_jaxpr/ppermute | solution.py:11
  44.6 11.6 %collective-permute-start = (f32[1,4,128,128]{3,2,1,0:T(8,128)S(1)}, f32[1,4,128,128]{3,2,1,0:T(8,128)S(1)}, u32[]{:S(2)}, u32[]{:S(2)}) collective-permute-start(f32[1,4,128,128]{3,2,1,0:T(8,128)S(1)} %fusion.21), channel_id=1, source_target_pairs={{0,1},{1,2},{2,3},{3,4},{4,5},{5,6},{6,7},{7,8},{8,9},{9,10},{10,1... | collective-permute-start | bytes 786440 | tf_op jit(solution)/shard_map/while/body/eval_jaxpr/ppermute | solution.py:11
  56.3 11.6 %collective-permute-start = (f32[1,4,128,128]{3,2,1,0:T(8,128)S(1)}, f32[1,4,128,128]{3,2,1,0:T(8,128)S(1)}, u32[]{:S(2)}, u32[]{:S(2)}) collective-permute-start(f32[1,4,128,128]{3,2,1,0:T(8,128)S(1)} %fusion.21), channel_id=1, source_target_pairs={{0,1},{1,2},{2,3},{3,4},{4,5},{5,6},{6,7},{7,8},{8,9},{9,10},{10,1... | collective-permute-start | bytes 786440 | tf_op jit(solution)/shard_map/while/body/eval_jaxpr/ppermute | solution.py:11
  68.0 11.6 %collective-permute-start = (f32[1,4,128,128]{3,2,1,0:T(8,128)S(1)}, f32[1,4,128,128]{3,2,1,0:T(8,128)S(1)}, u32[]{:S(2)}, u32[]{:S(2)}) collective-permute-start(f32[1,4,128,128]{3,2,1,0:T(8,128)S(1)} %fusion.21), channel_id=1, source_target_pairs={{0,1},{1,2},{2,3},{3,4},{4,5},{5,6},{6,7},{7,8},{8,9},{9,10},{10,1... | collective-permute-start | bytes 786440 | tf_op jit(solution)/shard_map/while/body/eval_jaxpr/ppermute | solution.py:11
  79.8 11.6 %collective-permute-start = (f32[1,4,128,128]{3,2,1,0:T(8,128)S(1)}, f32[1,4,128,128]{3,2,1,0:T(8,128)S(1)}, u32[]{:S(2)}, u32[]{:S(2)}) collective-permute-start(f32[1,4,128,128]{3,2,1,0:T(8,128)S(1)} %fusion.21), channel_id=1, source_target_pairs={{0,1},{1,2},{2,3},{3,4},{4,5},{5,6},{6,7},{7,8},{8,9},{9,10},{10,1... | collective-permute-start | bytes 786440 | tf_op jit(solution)/shard_map/while/body/eval_jaxpr/ppermute | solution.py:11
  91.5 11.6 %collective-permute-start = (f32[1,4,128,128]{3,2,1,0:T(8,128)S(1)}, f32[1,4,128,128]{3,2,1,0:T(8,128)S(1)}, u32[]{:S(2)}, u32[]{:S(2)}) collective-permute-start(f32[1,4,128,128]{3,2,1,0:T(8,128)S(1)} %fusion.21), channel_id=1, source_target_pairs={{0,1},{1,2},{2,3},{3,4},{4,5},{5,6},{6,7},{7,8},{8,9},{9,10},{10,1... | collective-permute-start | bytes 786440 | tf_op jit(solution)/shard_map/while/body/eval_jaxpr/ppermute | solution.py:11
  103.2 11.6 %collective-permute-start = (f32[1,4,128,128]{3,2,1,0:T(8,128)S(1)}, f32[1,4,128,128]{3,2,1,0:T(8,128)S(1)}, u32[]{:S(2)}, u32[]{:S(2)}) collective-permute-start(f32[1,4,128,128]{3,2,1,0:T(8,128)S(1)} %fusion.21), channel_id=1, source_target_pairs={{0,1},{1,2},{2,3},{3,4},{4,5},{5,6},{6,7},{7,8},{8,9},{9,10},{10,1... | collective-permute-start | bytes 786440 | tf_op jit(solution)/shard_map/while/body/eval_jaxpr/ppermute | solution.py:11
  115.0 11.6 %collective-permute-start = (f32[1,4,128,128]{3,2,1,0:T(8,128)S(1)}, f32[1,4,128,128]{3,2,1,0:T(8,128)S(1)}, u32[]{:S(2)}, u32[]{:S(2)}) collective-permute-start(f32[1,4,128,128]{3,2,1,0:T(8,128)S(1)} %fusion.21), channel_id=1, source_target_pairs={{0,1},{1,2},{2,3},{3,4},{4,5},{5,6},{6,7},{7,8},{8,9},{9,10},{10,1... | collective-permute-start | bytes 786440 | tf_op jit(solution)/shard_map/while/body/eval_jaxpr/ppermute | solution.py:11
  126.7 11.6 %collective-permute-start = (f32[1,4,128,128]{3,2,1,0:T(8,128)S(1)}, f32[1,4,128,128]{3,2,1,0:T(8,128)S(1)}, u32[]{:S(2)}, u32[]{:S(2)}) collective-permute-start(f32[1,4,128,128]{3,2,1,0:T(8,128)S(1)} %fusion.21), channel_id=1, source_target_pairs={{0,1},{1,2},{2,3},{3,4},{4,5},{5,6},{6,7},{7,8},{8,9},{9,10},{10,1... | collective-permute-start | bytes 786440 | tf_op jit(solution)/shard_map/while/body/eval_jaxpr/ppermute | solution.py:11
  138.4 11.6 %collective-permute-start = (f32[1,4,128,128]{3,2,1,0:T(8,128)S(1)}, f32[1,4,128,128]{3,2,1,0:T(8,128)S(1)}, u32[]{:S(2)}, u32[]{:S(2)}) collective-permute-start(f32[1,4,128,128]{3,2,1,0:T(8,128)S(1)} %fusion.21), channel_id=1, source_target_pairs={{0,1},{1,2},{2,3},{3,4},{4,5},{5,6},{6,7},{7,8},{8,9},{9,10},{10,1... | collective-permute-start | bytes 786440 | tf_op jit(solution)/shard_map/while/body/eval_jaxpr/ppermute | solution.py:11
  150.2 11.6 %collective-permute-start = (f32[1,4,128,128]{3,2,1,0:T(8,128)S(1)}, f32[1,4,128,128]{3,2,1,0:T(8,128)S(1)}, u32[]{:S(2)}, u32[]{:S(2)}) collective-permute-start(f32[1,4,128,128]{3,2,1,0:T(8,128)S(1)} %fusion.21), channel_id=1, source_target_pairs={{0,1},{1,2},{2,3},{3,4},{4,5},{5,6},{6,7},{7,8},{8,9},{9,10},{10,1... | collective-permute-start | bytes 786440 | tf_op jit(solution)/shard_map/while/body/eval_jaxpr/ppermute | solution.py:11
  161.9 11.6 %collective-permute-start = (f32[1,4,128,128]{3,2,1,0:T(8,128)S(1)}, f32[1,4,128,128]{3,2,1,0:T(8,128)S(1)}, u32[]{:S(2)}, u32[]{:S(2)}) collective-permute-start(f32[1,4,128,128]{3,2,1,0:T(8,128)S(1)} %fusion.21), channel_id=1, source_target_pairs={{0,1},{1,2},{2,3},{3,4},{4,5},{5,6},{6,7},{7,8},{8,9},{9,10},{10,1... | collective-permute-start | bytes 786440 | tf_op jit(solution)/shard_map/while/body/eval_jaxpr/ppermute | solution.py:11
  173.7 11.6 %collective-permute-start = (f32[1,4,128,128]{3,2,1,0:T(8,128)S(1)}, f32[1,4,128,128]{3,2,1,0:T(8,128)S(1)}, u32[]{:S(2)}, u32[]{:S(2)}) collective-permute-start(f32[1,4,128,128]{3,2,1,0:T(8,128)S(1)} %fusion.21), channel_id=1, source_target_pairs={{0,1},{1,2},{2,3},{3,4},{4,5},{5,6},{6,7},{7,8},{8,9},{9,10},{10,1... | collective-permute-start | bytes 786440 | tf_op jit(solution)/shard_map/while/body/eval_jaxpr/ppermute | solution.py:11
  185.4 11.6 %collective-permute-start = (f32[1,4,128,128]{3,2,1,0:T(8,128)S(1)}, f32[1,4,128,128]{3,2,1,0:T(8,128)S(1)}, u32[]{:S(2)}, u32[]{:S(2)}) collective-permute-start(f32[1,4,128,128]{3,2,1,0:T(8,128)S(1)} %fusion.21), channel_id=1, source_target_pairs={{0,1},{1,2},{2,3},{3,4},{4,5},{5,6},{6,7},{7,8},{8,9},{9,10},{10,1... | collective-permute-start | bytes 786440 | tf_op jit(solution)/shard_map/while/body/eval_jaxpr/ppermute | solution.py:11
  197.1 11.6 %collective-permute-start = (f32[1,4,128,128]{3,2,1,0:T(8,128)S(1)}, f32[1,4,128,128]{3,2,1,0:T(8,128)S(1)}, u32[]{:S(2)}, u32[]{:S(2)}) collective-permute-start(f32[1,4,128,128]{3,2,1,0:T(8,128)S(1)} %fusion.21), channel_id=1, source_target_pairs={{0,1},{1,2},{2,3},{3,4},{4,5},{5,6},{6,7},{7,8},{8,9},{9,10},{10,1... | collective-permute-start | bytes 786440 | tf_op jit(solution)/shard_map/while/body/eval_jaxpr/ppermute | solution.py:11
  208.9 11.6 %collective-permute-start = (f32[1,4,128,128]{3,2,1,0:T(8,128)S(1)}, f32[1,4,128,128]{3,2,1,0:T(8,128)S(1)}, u32[]{:S(2)}, u32[]{:S(2)}) collective-permute-start(f32[1,4,128,128]{3,2,1,0:T(8,128)S(1)} %fusion.21), channel_id=1, source_target_pairs={{0,1},{1,2},{2,3},{3,4},{4,5},{5,6},{6,7},{7,8},{8,9},{9,10},{10,1... | collective-permute-start | bytes 786440 | tf_op jit(solution)/shard_map/while/body/eval_jaxpr/ppermute | solution.py:11
  220.6 11.6 %collective-permute-start = (f32[1,4,128,128]{3,2,1,0:T(8,128)S(1)}, f32[1,4,128,128]{3,2,1,0:T(8,128)S(1)}, u32[]{:S(2)}, u32[]{:S(2)}) collective-permute-start(f32[1,4,128,128]{3,2,1,0:T(8,128)S(1)} %fusion.21), channel_id=1, source_target_pairs={{0,1},{1,2},{2,3},{3,4},{4,5},{5,6},{6,7},{7,8},{8,9},{9,10},{10,1... | collective-permute-start | bytes 786440 | tf_op jit(solution)/shard_map/while/body/eval_jaxpr/ppermute | solution.py:11
  232.3 11.6 %collective-permute-start = (f32[1,4,128,128]{3,2,1,0:T(8,128)S(1)}, f32[1,4,128,128]{3,2,1,0:T(8,128)S(1)}, u32[]{:S(2)}, u32[]{:S(2)}) collective-permute-start(f32[1,4,128,128]{3,2,1,0:T(8,128)S(1)} %fusion.21), channel_id=1, source_target_pairs={{0,1},{1,2},{2,3},{3,4},{4,5},{5,6},{6,7},{7,8},{8,9},{9,10},{10,1... | collective-permute-start | bytes 786440 | tf_op jit(solution)/shard_map/while/body/eval_jaxpr/ppermute | solution.py:11
  244.1 11.6 %collective-permute-start = (f32[1,4,128,128]{3,2,1,0:T(8,128)S(1)}, f32[1,4,128,128]{3,2,1,0:T(8,128)S(1)}, u32[]{:S(2)}, u32[]{:S(2)}) collective-permute-start(f32[1,4,128,128]{3,2,1,0:T(8,128)S(1)} %fusion.21), channel_id=1, source_target_pairs={{0,1},{1,2},{2,3},{3,4},{4,5},{5,6},{6,7},{7,8},{8,9},{9,10},{10,1... | collective-permute-start | bytes 786440 | tf_op jit(solution)/shard_map/while/body/eval_jaxpr/ppermute | solution.py:11
  255.8 11.6 %collective-permute-start = (f32[1,4,128,128]{3,2,1,0:T(8,128)S(1)}, f32[1,4,128,128]{3,2,1,0:T(8,128)S(1)}, u32[]{:S(2)}, u32[]{:S(2)}) collective-permute-start(f32[1,4,128,128]{3,2,1,0:T(8,128)S(1)} %fusion.21), channel_id=1, source_target_pairs={{0,1},{1,2},{2,3},{3,4},{4,5},{5,6},{6,7},{7,8},{8,9},{9,10},{10,1... | collective-permute-start | bytes 786440 | tf_op jit(solution)/shard_map/while/body/eval_jaxpr/ppermute | solution.py:11
  267.5 11.6 %collective-permute-start = (f32[1,4,128,128]{3,2,1,0:T(8,128)S(1)}, f32[1,4,128,128]{3,2,1,0:T(8,128)S(1)}, u32[]{:S(2)}, u32[]{:S(2)}) collective-permute-start(f32[1,4,128,128]{3,2,1,0:T(8,128)S(1)} %fusion.21), channel_id=1, source_target_pairs={{0,1},{1,2},{2,3},{3,4},{4,5},{5,6},{6,7},{7,8},{8,9},{9,10},{10,1... | collective-permute-start | bytes 786440 | tf_op jit(solution)/shard_map/while/body/eval_jaxpr/ppermute | solution.py:11
  279.3 11.6 %collective-permute-start = (f32[1,4,128,128]{3,2,1,0:T(8,128)S(1)}, f32[1,4,128,128]{3,2,1,0:T(8,128)S(1)}, u32[]{:S(2)}, u32[]{:S(2)}) collective-permute-start(f32[1,4,128,128]{3,2,1,0:T(8,128)S(1)} %fusion.21), channel_id=1, source_target_pairs={{0,1},{1,2},{2,3},{3,4},{4,5},{5,6},{6,7},{7,8},{8,9},{9,10},{10,1... | collective-permute-start | bytes 786440 | tf_op jit(solution)/shard_map/while/body/eval_jaxpr/ppermute | solution.py:11
  291.0 11.6 %collective-permute-start = (f32[1,4,128,128]{3,2,1,0:T(8,128)S(1)}, f32[1,4,128,128]{3,2,1,0:T(8,128)S(1)}, u32[]{:S(2)}, u32[]{:S(2)}) collective-permute-start(f32[1,4,128,128]{3,2,1,0:T(8,128)S(1)} %fusion.21), channel_id=1, source_target_pairs={{0,1},{1,2},{2,3},{3,4},{4,5},{5,6},{6,7},{7,8},{8,9},{9,10},{10,1... | collective-permute-start | bytes 786440 | tf_op jit(solution)/shard_map/while/body/eval_jaxpr/ppermute | solution.py:11
  302.7 11.6 %collective-permute-start = (f32[1,4,128,128]{3,2,1,0:T(8,128)S(1)}, f32[1,4,128,128]{3,2,1,0:T(8,128)S(1)}, u32[]{:S(2)}, u32[]{:S(2)}) collective-permute-start(f32[1,4,128,128]{3,2,1,0:T(8,128)S(1)} %fusion.21), channel_id=1, source_target_pairs={{0,1},{1,2},{2,3},{3,4},{4,5},{5,6},{6,7},{7,8},{8,9},{9,10},{10,1... | collective-permute-start | bytes 786440 | tf_op jit(solution)/shard_map/while/body/eval_jaxpr/ppermute | solution.py:11
  314.5 11.6 %collective-permute-start = (f32[1,4,128,128]{3,2,1,0:T(8,128)S(1)}, f32[1,4,128,128]{3,2,1,0:T(8,128)S(1)}, u32[]{:S(2)}, u32[]{:S(2)}) collective-permute-start(f32[1,4,128,128]{3,2,1,0:T(8,128)S(1)} %fusion.21), channel_id=1, source_target_pairs={{0,1},{1,2},{2,3},{3,4},{4,5},{5,6},{6,7},{7,8},{8,9},{9,10},{10,1... | collective-permute-start | bytes 786440 | tf_op jit(solution)/shard_map/while/body/eval_jaxpr/ppermute | solution.py:11
  326.2 11.6 %collective-permute-start = (f32[1,4,128,128]{3,2,1,0:T(8,128)S(1)}, f32[1,4,128,128]{3,2,1,0:T(8,128)S(1)}, u32[]{:S(2)}, u32[]{:S(2)}) collective-permute-start(f32[1,4,128,128]{3,2,1,0:T(8,128)S(1)} %fusion.21), channel_id=1, source_target_pairs={{0,1},{1,2},{2,3},{3,4},{4,5},{5,6},{6,7},{7,8},{8,9},{9,10},{10,1... | collective-permute-start | bytes 786440 | tf_op jit(solution)/shard_map/while/body/eval_jaxpr/ppermute | solution.py:11
  337.9 11.6 %collective-permute-start = (f32[1,4,128,128]{3,2,1,0:T(8,128)S(1)}, f32[1,4,128,128]{3,2,1,0:T(8,128)S(1)}, u32[]{:S(2)}, u32[]{:S(2)}) collective-permute-start(f32[1,4,128,128]{3,2,1,0:T(8,128)S(1)} %fusion.21), channel_id=1, source_target_pairs={{0,1},{1,2},{2,3},{3,4},{4,5},{5,6},{6,7},{7,8},{8,9},{9,10},{10,1... | collective-permute-start | bytes 786440 | tf_op jit(solution)/shard_map/while/body/eval_jaxpr/ppermute | solution.py:11
  349.7 11.6 %collective-permute-start = (f32[1,4,128,128]{3,2,1,0:T(8,128)S(1)}, f32[1,4,128,128]{3,2,1,0:T(8,128)S(1)}, u32[]{:S(2)}, u32[]{:S(2)}) collective-permute-start(f32[1,4,128,128]{3,2,1,0:T(8,128)S(1)} %fusion.21), channel_id=1, source_target_pairs={{0,1},{1,2},{2,3},{3,4},{4,5},{5,6},{6,7},{7,8},{8,9},{9,10},{10,1... | collective-permute-start | bytes 786440 | tf_op jit(solution)/shard_map/while/body/eval_jaxpr/ppermute | solution.py:11
  361.4 11.7 %collective-permute-start = (f32[1,4,128,128]{3,2,1,0:T(8,128)S(1)}, f32[1,4,128,128]{3,2,1,0:T(8,128)S(1)}, u32[]{:S(2)}, u32[]{:S(2)}) collective-permute-start(f32[1,4,128,128]{3,2,1,0:T(8,128)S(1)} %fusion.21), channel_id=1, source_target_pairs={{0,1},{1,2},{2,3},{3,4},{4,5},{5,6},{6,7},{7,8},{8,9},{9,10},{10,1... | collective-permute-start | bytes 786440 | tf_op jit(solution)/shard_map/while/body/eval_jaxpr/ppermute | solution.py:11
  387.5 59.9 %copy-start.2 = (f32[512]{0:T(512)S(1)}, f32[512]{0:T(512)}, u32[]{:S(2)}) copy-start(f32[512]{0:T(512)} %param.12) | copy-start | bytes 6148
  (2 other events, 9.0 us)
where the time goes:
time: 451 us; the launch traced here: 450 us
  waiting for transfers between devices  302 us (67%)
  starting transfers between devices  59.5 us (13%)
  blocking collectives  54 us (12%)
  matrix products  15.3 us (3%)
  other arithmetic  11.8 us (3%)
  local copies, waits for them, and re-layouts  5.88 us (1%)
    ppermute x31, waiting for transfers between devices, from_behind(): lax.ppermute(shard, axis, [(i, (i + by) % count) for i in range(count)])  302 us
    ppermute x31, starting transfers between devices, from_behind(): lax.ppermute(shard, axis, [(i, (i + by) % count) for i in range(count)])  59.5 us
    psum x1, blocking collectives, body(): sum_squares = lax.psum(squares, 'head')  54 us
    dot_general x1, matrix products, body(): jnp.einsum('shij,sjhd->sihd', weights, value_heads, preferred_element_typ...  9.53 us
  transfers between devices with their start and end apart: 31, of which 31 were waited for; matrix products, arithmetic and copies ran while one was open for 0% of the time, Pallas kernels for 0%

commit v1 on v0

--- a/solution.py
+++ b/solution.py
@@ -59,7 +59,7 @@
     )
     attended = (inner_part + carried_part).reshape(seq_count, block_len, columns)
     squares = jnp.sum(attended * attended, axis=-1)
-    sum_squares = lax.psum(squares, "head")
+    sum_squares = jnp.sum(lax.all_gather(squares, "head"), axis=0)
     features_all = columns * lax.axis_size("head")
     inv_rms = lax.rsqrt(sum_squares / features_all + epsilon)
     return (attended * inv_rms[..., None] * norm_gain).astype(jnp.bfloat16)

time: 451 us -> 448 us (level)
    psum x1 -> x0, blocking collectives: 54 us -> none  [body(): sum_squares = lax.psum(squares, 'head')]
    all_gather x0 -> x1, blocking collectives: none -> 53.2 us  [body(): sum_squares = jnp.sum(lax.all_gather(squares, 'head'), axis=0)]
where the time goes in v1:
time: 448 us; the launch traced here: 447 us
  waiting for transfers between devices  302 us (67%)
  starting transfers between devices  59.5 us (13%)
  blocking collectives  53.2 us (12%)
  matrix products  14.6 us (3%)
  other arithmetic  10.2 us (2%)
  local copies, waits for them, and re-layouts  6 us (1%)
    ppermute x31, waiting for transfers between devices, from_behind(): lax.ppermute(shard, axis, [(i, (i + by) % count) for i in range(count)])  302 us
    ppermute x31, starting transfers between devices, from_behind(): lax.ppermute(shard, axis, [(i, (i + by) % count) for i in range(count)])  59.5 us
    all_gather x1, blocking collectives, body(): sum_squares = jnp.sum(lax.all_gather(squares, 'head'), axis=0)  53.2 us
    dot_general x1, matrix products, body(): jnp.einsum('shij,sjhd->sihd', weights, value_heads, preferred_element_typ...  9.08 us
  transfers between devices with their start and end apart: 31, of which 31 were waited for; matrix products, arithmetic and copies ran while one was open for 0% of the time, Pallas kernels for 0%

profile of v1, /device:TPU:8, one launch (start us, length us, event | category | flops | bytes accessed | tf_op | source)
XLA Modules:
  0.0 447.4 jit_solution(16749843118698268623)
XLA Ops:
  7.3 365.9 %while.13 = (s32[]{:T(128)}, f32[1,4,128,128]{3,2,1,0:T(8,128)S(1)}, pred[1]{0:T(512)(128)(4,1)}, f32[1,4,1,1]{1,3,2,0:T(1,128)S(1)}, f32[1,4,128,128]{3,2,1,0:T(8,128)S(1)}, /*index=5*/s32[]{:T(128)}, s32[]{:T(128)}) while((s32[]{:T(128)}, f32[1,4,128,128]{3,2,1,0:T(8,128)S(1)}, pred[1]{0:T(512)(128)(4,1)}, ...), condition=%wide.region_1.2_spmd.clone, body=%wide.region_0.1_spmd.clone.sunk | while | flops 262148 | bytes 2359448 | solution.py:54
  9.4 11.7 %collective-permute-done = f32[1,4,128,128]{3,2,1,0:T(8,128)S(1)} collective-permute-done((f32[1,4,128,128]{3,2,1,0:T(8,128)S(1)}, f32[1,4,128,128]{3,2,1,0:T(8,128)S(1)}, u32[]{:S(2)}, u32[]{:S(2)}) %collective-permute-start) | collective-permute-done | bytes 262176 | tf_op jit(solution)/shard_map/while/body/eval_jaxpr/ppermute | solution.py:11
  23.1 9.7 %collective-permute-done = f32[1,4,128,128]{3,2,1,0:T(8,128)S(1)} collective-permute-done((f32[1,4,128,128]{3,2,1,0:T(8,128)S(1)}, f32[1,4,128,128]{3,2,1,0:T(8,128)S(1)}, u32[]{:S(2)}, u32[]{:S(2)}) %collective-permute-start) | collective-permute-done | bytes 262176 | tf_op jit(solution)/shard_map/while/body/eval_jaxpr/ppermute | solution.py:11
  34.8 9.7 %collective-permute-done = f32[1,4,128,128]{3,2,1,0:T(8,128)S(1)} collective-permute-done((f32[1,4,128,128]{3,2,1,0:T(8,128)S(1)}, f32[1,4,128,128]{3,2,1,0:T(8,128)S(1)}, u32[]{:S(2)}, u32[]{:S(2)}) %collective-permute-start) | collective-permute-done | bytes 262176 | tf_op jit(solution)/shard_map/while/body/eval_jaxpr/ppermute | solution.py:11
  46.6 9.7 %collective-permute-done = f32[1,4,128,128]{3,2,1,0:T(8,128)S(1)} collective-permute-done((f32[1,4,128,128]{3,2,1,0:T(8,128)S(1)}, f32[1,4,128,128]{3,2,1,0:T(8,128)S(1)}, u32[]{:S(2)}, u32[]{:S(2)}) %collective-permute-start) | collective-permute-done | bytes 262176 | tf_op jit(solution)/shard_map/while/body/eval_jaxpr/ppermute | solution.py:11
  58.3 9.7 %collective-permute-done = f32[1,4,128,128]{3,2,1,0:T(8,128)S(1)} collective-permute-done((f32[1,4,128,128]{3,2,1,0:T(8,128)S(1)}, f32[1,4,128,128]{3,2,1,0:T(8,128)S(1)}, u32[]{:S(2)}, u32[]{:S(2)}) %collective-permute-start) | collective-permute-done | bytes 262176 | tf_op jit(solution)/shard_map/while/body/eval_jaxpr/ppermute | solution.py:11
  70.0 9.7 %collective-permute-done = f32[1,4,128,128]{3,2,1,0:T(8,128)S(1)} collective-permute-done((f32[1,4,128,128]{3,2,1,0:T(8,128)S(1)}, f32[1,4,128,128]{3,2,1,0:T(8,128)S(1)}, u32[]{:S(2)}, u32[]{:S(2)}) %collective-permute-start) | collective-permute-done | bytes 262176 | tf_op jit(solution)/shard_map/while/body/eval_jaxpr/ppermute | solution.py:11
  81.8 9.7 %collective-permute-done = f32[1,4,128,128]{3,2,1,0:T(8,128)S(1)} collective-permute-done((f32[1,4,128,128]{3,2,1,0:T(8,128)S(1)}, f32[1,4,128,128]{3,2,1,0:T(8,128)S(1)}, u32[]{:S(2)}, u32[]{:S(2)}) %collective-permute-start) | collective-permute-done | bytes 262176 | tf_op jit(solution)/shard_map/while/body/eval_jaxpr/ppermute | solution.py:11
  93.5 9.7 %collective-permute-done = f32[1,4,128,128]{3,2,1,0:T(8,128)S(1)} collective-permute-done((f32[1,4,128,128]{3,2,1,0:T(8,128)S(1)}, f32[1,4,128,128]{3,2,1,0:T(8,128)S(1)}, u32[]{:S(2)}, u32[]{:S(2)}) %collective-permute-start) | collective-permute-done | bytes 262176 | tf_op jit(solution)/shard_map/while/body/eval_jaxpr/ppermute | solution.py:11
  105.2 9.7 %collective-permute-done = f32[1,4,128,128]{3,2,1,0:T(8,128)S(1)} collective-permute-done((f32[1,4,128,128]{3,2,1,0:T(8,128)S(1)}, f32[1,4,128,128]{3,2,1,0:T(8,128)S(1)}, u32[]{:S(2)}, u32[]{:S(2)}) %collective-permute-start) | collective-permute-done | bytes 262176 | tf_op jit(solution)/shard_map/while/body/eval_jaxpr/ppermute | solution.py:11
  117.0 9.7 %collective-permute-done = f32[1,4,128,128]{3,2,1,0:T(8,128)S(1)} collective-permute-done((f32[1,4,128,128]{3,2,1,0:T(8,128)S(1)}, f32[1,4,128,128]{3,2,1,0:T(8,128)S(1)}, u32[]{:S(2)}, u32[]{:S(2)}) %collective-permute-start) | collective-permute-done | bytes 262176 | tf_op jit(solution)/shard_map/while/body/eval_jaxpr/ppermute | solution.py:11
  128.7 9.7 %collective-permute-done = f32[1,4,128,128]{3,2,1,0:T(8,128)S(1)} collective-permute-done((f32[1,4,128,128]{3,2,1,0:T(8,128)S(1)}, f32[1,4,128,128]{3,2,1,0:T(8,128)S(1)}, u32[]{:S(2)}, u32[]{:S(2)}) %collective-permute-start) | collective-permute-done | bytes 262176 | tf_op jit(solution)/shard_map/while/body/eval_jaxpr/ppermute | solution.py:11
  140.4 9.7 %collective-permute-done = f32[1,4,128,128]{3,2,1,0:T(8,128)S(1)} collective-permute-done((f32[1,4,128,128]{3,2,1,0:T(8,128)S(1)}, f32[1,4,128,128]{3,2,1,0:T(8,128)S(1)}, u32[]{:S(2)}, u32[]{:S(2)}) %collective-permute-start) | collective-permute-done | bytes 262176 | tf_op jit(solution)/shard_map/while/body/eval_jaxpr/ppermute | solution.py:11
  152.2 9.7 %collective-permute-done = f32[1,4,128,128]{3,2,1,0:T(8,128)S(1)} collective-permute-done((f32[1,4,128,128]{3,2,1,0:T(8,128)S(1)}, f32[1,4,128,128]{3,2,1,0:T(8,128)S(1)}, u32[]{:S(2)}, u32[]{:S(2)}) %collective-permute-start) | collective-permute-done | bytes 262176 | tf_op jit(solution)/shard_map/while/body/eval_jaxpr/ppermute | solution.py:11
  163.9 9.7 %collective-permute-done = f32[1,4,128,128]{3,2,1,0:T(8,128)S(1)} collective-permute-done((f32[1,4,128,128]{3,2,1,0:T(8,128)S(1)}, f32[1,4,128,128]{3,2,1,0:T(8,128)S(1)}, u32[]{:S(2)}, u32[]{:S(2)}) %collective-permute-start) | collective-permute-done | bytes 262176 | tf_op jit(solution)/shard_map/while/body/eval_jaxpr/ppermute | solution.py:11
  175.6 9.7 %collective-permute-done = f32[1,4,128,128]{3,2,1,0:T(8,128)S(1)} collective-permute-done((f32[1,4,128,128]{3,2,1,0:T(8,128)S(1)}, f32[1,4,128,128]{3,2,1,0:T(8,128)S(1)}, u32[]{:S(2)}, u32[]{:S(2)}) %collective-permute-start) | collective-permute-done | bytes 262176 | tf_op jit(solution)/shard_map/while/body/eval_jaxpr/ppermute | solution.py:11
  187.4 9.7 %collective-permute-done = f32[1,4,128,128]{3,2,1,0:T(8,128)S(1)} collective-permute-done((f32[1,4,128,128]{3,2,1,0:T(8,128)S(1)}, f32[1,4,128,128]{3,2,1,0:T(8,128)S(1)}, u32[]{:S(2)}, u32[]{:S(2)}) %collective-permute-start) | collective-permute-done | bytes 262176 | tf_op jit(solution)/shard_map/while/body/eval_jaxpr/ppermute | solution.py:11
  199.1 9.7 %collective-permute-done = f32[1,4,128,128]{3,2,1,0:T(8,128)S(1)} collective-permute-done((f32[1,4,128,128]{3,2,1,0:T(8,128)S(1)}, f32[1,4,128,128]{3,2,1,0:T(8,128)S(1)}, u32[]{:S(2)}, u32[]{:S(2)}) %collective-permute-start) | collective-permute-done | bytes 262176 | tf_op jit(solution)/shard_map/while/body/eval_jaxpr/ppermute | solution.py:11
  210.9 9.7 %collective-permute-done = f32[1,4,128,128]{3,2,1,0:T(8,128)S(1)} collective-permute-done((f32[1,4,128,128]{3,2,1,0:T(8,128)S(1)}, f32[1,4,128,128]{3,2,1,0:T(8,128)S(1)}, u32[]{:S(2)}, u32[]{:S(2)}) %collective-permute-start) | collective-permute-done | bytes 262176 | tf_op jit(solution)/shard_map/while/body/eval_jaxpr/ppermute | solution.py:11
  222.6 9.7 %collective-permute-done = f32[1,4,128,128]{3,2,1,0:T(8,128)S(1)} collective-permute-done((f32[1,4,128,128]{3,2,1,0:T(8,128)S(1)}, f32[1,4,128,128]{3,2,1,0:T(8,128)S(1)}, u32[]{:S(2)}, u32[]{:S(2)}) %collective-permute-start) | collective-permute-done | bytes 262176 | tf_op jit(solution)/shard_map/while/body/eval_jaxpr/ppermute | solution.py:11
  234.3 9.7 %collective-permute-done = f32[1,4,128,128]{3,2,1,0:T(8,128)S(1)} collective-permute-done((f32[1,4,128,128]{3,2,1,0:T(8,128)S(1)}, f32[1,4,128,128]{3,2,1,0:T(8,128)S(1)}, u32[]{:S(2)}, u32[]{:S(2)}) %collective-permute-start) | collective-permute-done | bytes 262176 | tf_op jit(solution)/shard_map/while/body/eval_jaxpr/ppermute | solution.py:11
  246.1 9.7 %collective-permute-done = f32[1,4,128,128]{3,2,1,0:T(8,128)S(1)} collective-permute-done((f32[1,4,128,128]{3,2,1,0:T(8,128)S(1)}, f32[1,4,128,128]{3,2,1,0:T(8,128)S(1)}, u32[]{:S(2)}, u32[]{:S(2)}) %collective-permute-start) | collective-permute-done | bytes 262176 | tf_op jit(solution)/shard_map/while/body/eval_jaxpr/ppermute | solution.py:11
  257.8 9.7 %collective-permute-done = f32[1,4,128,128]{3,2,1,0:T(8,128)S(1)} collective-permute-done((f32[1,4,128,128]{3,2,1,0:T(8,128)S(1)}, f32[1,4,128,128]{3,2,1,0:T(8,128)S(1)}, u32[]{:S(2)}, u32[]{:S(2)}) %collective-permute-start) | collective-permute-done | bytes 262176 | tf_op jit(solution)/shard_map/while/body/eval_jaxpr/ppermute | solution.py:11
  269.5 9.7 %collective-permute-done = f32[1,4,128,128]{3,2,1,0:T(8,128)S(1)} collective-permute-done((f32[1,4,128,128]{3,2,1,0:T(8,128)S(1)}, f32[1,4,128,128]{3,2,1,0:T(8,128)S(1)}, u32[]{:S(2)}, u32[]{:S(2)}) %collective-permute-start) | collective-permute-done | bytes 262176 | tf_op jit(solution)/shard_map/while/body/eval_jaxpr/ppermute | solution.py:11
  281.3 9.7 %collective-permute-done = f32[1,4,128,128]{3,2,1,0:T(8,128)S(1)} collective-permute-done((f32[1,4,128,128]{3,2,1,0:T(8,128)S(1)}, f32[1,4,128,128]{3,2,1,0:T(8,128)S(1)}, u32[]{:S(2)}, u32[]{:S(2)}) %collective-permute-start) | collective-permute-done | bytes 262176 | tf_op jit(solution)/shard_map/while/body/eval_jaxpr/ppermute | solution.py:11
  293.0 9.7 %collective-permute-done = f32[1,4,128,128]{3,2,1,0:T(8,128)S(1)} collective-permute-done((f32[1,4,128,128]{3,2,1,0:T(8,128)S(1)}, f32[1,4,128,128]{3,2,1,0:T(8,128)S(1)}, u32[]{:S(2)}, u32[]{:S(2)}) %collective-permute-start) | collective-permute-done | bytes 262176 | tf_op jit(solution)/shard_map/while/body/eval_jaxpr/ppermute | solution.py:11
  304.7 9.7 %collective-permute-done = f32[1,4,128,128]{3,2,1,0:T(8,128)S(1)} collective-permute-done((f32[1,4,128,128]{3,2,1,0:T(8,128)S(1)}, f32[1,4,128,128]{3,2,1,0:T(8,128)S(1)}, u32[]{:S(2)}, u32[]{:S(2)}) %collective-permute-start) | collective-permute-done | bytes 262176 | tf_op jit(solution)/shard_map/while/body/eval_jaxpr/ppermute | solution.py:11
  316.5 9.7 %collective-permute-done = f32[1,4,128,128]{3,2,1,0:T(8,128)S(1)} collective-permute-done((f32[1,4,128,128]{3,2,1,0:T(8,128)S(1)}, f32[1,4,128,128]{3,2,1,0:T(8,128)S(1)}, u32[]{:S(2)}, u32[]{:S(2)}) %collective-permute-start) | collective-permute-done | bytes 262176 | tf_op jit(solution)/shard_map/while/body/eval_jaxpr/ppermute | solution.py:11
  328.2 9.7 %collective-permute-done = f32[1,4,128,128]{3,2,1,0:T(8,128)S(1)} collective-permute-done((f32[1,4,128,128]{3,2,1,0:T(8,128)S(1)}, f32[1,4,128,128]{3,2,1,0:T(8,128)S(1)}, u32[]{:S(2)}, u32[]{:S(2)}) %collective-permute-start) | collective-permute-done | bytes 262176 | tf_op jit(solution)/shard_map/while/body/eval_jaxpr/ppermute | solution.py:11
  339.9 9.7 %collective-permute-done = f32[1,4,128,128]{3,2,1,0:T(8,128)S(1)} collective-permute-done((f32[1,4,128,128]{3,2,1,0:T(8,128)S(1)}, f32[1,4,128,128]{3,2,1,0:T(8,128)S(1)}, u32[]{:S(2)}, u32[]{:S(2)}) %collective-permute-start) | collective-permute-done | bytes 262176 | tf_op jit(solution)/shard_map/while/body/eval_jaxpr/ppermute | solution.py:11
  363.4 9.8 %collective-permute-done = f32[1,4,128,128]{3,2,1,0:T(8,128)S(1)} collective-permute-done((f32[1,4,128,128]{3,2,1,0:T(8,128)S(1)}, f32[1,4,128,128]{3,2,1,0:T(8,128)S(1)}, u32[]{:S(2)}, u32[]{:S(2)}) %collective-permute-start) | collective-permute-done | bytes 262176 | tf_op jit(solution)/shard_map/while/body/eval_jaxpr/ppermute | solution.py:11
  392.8 53.2 %all-gather = f32[16384]{0:T(1024)S(1)} all-gather(f32[1024]{0:T(1024)S(1)} %get-tuple-element.99), channel_id=2, replica_groups=mesh['head'=16,'seq'=32] {'head'}, dimensions={0}, use_global_device_ids=true | all-gather | bytes 69632 | tf_op jit(solution)/shard_map/all_gather | solution.py:62
  (118 shorter events, 100.0 us)
Async XLA Ops:
  7.4 13.6 %collective-permute-start = (f32[1,4,128,128]{3,2,1,0:T(8,128)S(1)}, f32[1,4,128,128]{3,2,1,0:T(8,128)S(1)}, u32[]{:S(2)}, u32[]{:S(2)}) collective-permute-start(f32[1,4,128,128]{3,2,1,0:T(8,128)S(1)} %fusion.21), channel_id=1, source_target_pairs={{0,1},{1,2},{2,3},{3,4},{4,5},{5,6},{6,7},{7,8},{8,9},{9,10},{10,1... | collective-permute-start | bytes 786440 | tf_op jit(solution)/shard_map/while/body/eval_jaxpr/ppermute | solution.py:11
  21.2 11.6 %collective-permute-start = (f32[1,4,128,128]{3,2,1,0:T(8,128)S(1)}, f32[1,4,128,128]{3,2,1,0:T(8,128)S(1)}, u32[]{:S(2)}, u32[]{:S(2)}) collective-permute-start(f32[1,4,128,128]{3,2,1,0:T(8,128)S(1)} %fusion.21), channel_id=1, source_target_pairs={{0,1},{1,2},{2,3},{3,4},{4,5},{5,6},{6,7},{7,8},{8,9},{9,10},{10,1... | collective-permute-start | bytes 786440 | tf_op jit(solution)/shard_map/while/body/eval_jaxpr/ppermute | solution.py:11
  32.9 11.6 %collective-permute-start = (f32[1,4,128,128]{3,2,1,0:T(8,128)S(1)}, f32[1,4,128,128]{3,2,1,0:T(8,128)S(1)}, u32[]{:S(2)}, u32[]{:S(2)}) collective-permute-start(f32[1,4,128,128]{3,2,1,0:T(8,128)S(1)} %fusion.21), channel_id=1, source_target_pairs={{0,1},{1,2},{2,3},{3,4},{4,5},{5,6},{6,7},{7,8},{8,9},{9,10},{10,1... | collective-permute-start | bytes 786440 | tf_op jit(solution)/shard_map/while/body/eval_jaxpr/ppermute | solution.py:11
  44.6 11.6 %collective-permute-start = (f32[1,4,128,128]{3,2,1,0:T(8,128)S(1)}, f32[1,4,128,128]{3,2,1,0:T(8,128)S(1)}, u32[]{:S(2)}, u32[]{:S(2)}) collective-permute-start(f32[1,4,128,128]{3,2,1,0:T(8,128)S(1)} %fusion.21), channel_id=1, source_target_pairs={{0,1},{1,2},{2,3},{3,4},{4,5},{5,6},{6,7},{7,8},{8,9},{9,10},{10,1... | collective-permute-start | bytes 786440 | tf_op jit(solution)/shard_map/while/body/eval_jaxpr/ppermute | solution.py:11
  56.4 11.6 %collective-permute-start = (f32[1,4,128,128]{3,2,1,0:T(8,128)S(1)}, f32[1,4,128,128]{3,2,1,0:T(8,128)S(1)}, u32[]{:S(2)}, u32[]{:S(2)}) collective-permute-start(f32[1,4,128,128]{3,2,1,0:T(8,128)S(1)} %fusion.21), channel_id=1, source_target_pairs={{0,1},{1,2},{2,3},{3,4},{4,5},{5,6},{6,7},{7,8},{8,9},{9,10},{10,1... | collective-permute-start | bytes 786440 | tf_op jit(solution)/shard_map/while/body/eval_jaxpr/ppermute | solution.py:11
  68.1 11.6 %collective-permute-start = (f32[1,4,128,128]{3,2,1,0:T(8,128)S(1)}, f32[1,4,128,128]{3,2,1,0:T(8,128)S(1)}, u32[]{:S(2)}, u32[]{:S(2)}) collective-permute-start(f32[1,4,128,128]{3,2,1,0:T(8,128)S(1)} %fusion.21), channel_id=1, source_target_pairs={{0,1},{1,2},{2,3},{3,4},{4,5},{5,6},{6,7},{7,8},{8,9},{9,10},{10,1... | collective-permute-start | bytes 786440 | tf_op jit(solution)/shard_map/while/body/eval_jaxpr/ppermute | solution.py:11
  79.8 11.6 %collective-permute-start = (f32[1,4,128,128]{3,2,1,0:T(8,128)S(1)}, f32[1,4,128,128]{3,2,1,0:T(8,128)S(1)}, u32[]{:S(2)}, u32[]{:S(2)}) collective-permute-start(f32[1,4,128,128]{3,2,1,0:T(8,128)S(1)} %fusion.21), channel_id=1, source_target_pairs={{0,1},{1,2},{2,3},{3,4},{4,5},{5,6},{6,7},{7,8},{8,9},{9,10},{10,1... | collective-permute-start | bytes 786440 | tf_op jit(solution)/shard_map/while/body/eval_jaxpr/ppermute | solution.py:11
  91.6 11.6 %collective-permute-start = (f32[1,4,128,128]{3,2,1,0:T(8,128)S(1)}, f32[1,4,128,128]{3,2,1,0:T(8,128)S(1)}, u32[]{:S(2)}, u32[]{:S(2)}) collective-permute-start(f32[1,4,128,128]{3,2,1,0:T(8,128)S(1)} %fusion.21), channel_id=1, source_target_pairs={{0,1},{1,2},{2,3},{3,4},{4,5},{5,6},{6,7},{7,8},{8,9},{9,10},{10,1... | collective-permute-start | bytes 786440 | tf_op jit(solution)/shard_map/while/body/eval_jaxpr/ppermute | solution.py:11
  103.3 11.6 %collective-permute-start = (f32[1,4,128,128]{3,2,1,0:T(8,128)S(1)}, f32[1,4,128,128]{3,2,1,0:T(8,128)S(1)}, u32[]{:S(2)}, u32[]{:S(2)}) collective-permute-start(f32[1,4,128,128]{3,2,1,0:T(8,128)S(1)} %fusion.21), channel_id=1, source_target_pairs={{0,1},{1,2},{2,3},{3,4},{4,5},{5,6},{6,7},{7,8},{8,9},{9,10},{10,1... | collective-permute-start | bytes 786440 | tf_op jit(solution)/shard_map/while/body/eval_jaxpr/ppermute | solution.py:11
  115.0 11.6 %collective-permute-start = (f32[1,4,128,128]{3,2,1,0:T(8,128)S(1)}, f32[1,4,128,128]{3,2,1,0:T(8,128)S(1)}, u32[]{:S(2)}, u32[]{:S(2)}) collective-permute-start(f32[1,4,128,128]{3,2,1,0:T(8,128)S(1)} %fusion.21), channel_id=1, source_target_pairs={{0,1},{1,2},{2,3},{3,4},{4,5},{5,6},{6,7},{7,8},{8,9},{9,10},{10,1... | collective-permute-start | bytes 786440 | tf_op jit(solution)/shard_map/while/body/eval_jaxpr/ppermute | solution.py:11
  126.8 11.6 %collective-permute-start = (f32[1,4,128,128]{3,2,1,0:T(8,128)S(1)}, f32[1,4,128,128]{3,2,1,0:T(8,128)S(1)}, u32[]{:S(2)}, u32[]{:S(2)}) collective-permute-start(f32[1,4,128,128]{3,2,1,0:T(8,128)S(1)} %fusion.21), channel_id=1, source_target_pairs={{0,1},{1,2},{2,3},{3,4},{4,5},{5,6},{6,7},{7,8},{8,9},{9,10},{10,1... | collective-permute-start | bytes 786440 | tf_op jit(solution)/shard_map/while/body/eval_jaxpr/ppermute | solution.py:11
  138.5 11.6 %collective-permute-start = (f32[1,4,128,128]{3,2,1,0:T(8,128)S(1)}, f32[1,4,128,128]{3,2,1,0:T(8,128)S(1)}, u32[]{:S(2)}, u32[]{:S(2)}) collective-permute-start(f32[1,4,128,128]{3,2,1,0:T(8,128)S(1)} %fusion.21), channel_id=1, source_target_pairs={{0,1},{1,2},{2,3},{3,4},{4,5},{5,6},{6,7},{7,8},{8,9},{9,10},{10,1... | collective-permute-start | bytes 786440 | tf_op jit(solution)/shard_map/while/body/eval_jaxpr/ppermute | solution.py:11
  150.2 11.6 %collective-permute-start = (f32[1,4,128,128]{3,2,1,0:T(8,128)S(1)}, f32[1,4,128,128]{3,2,1,0:T(8,128)S(1)}, u32[]{:S(2)}, u32[]{:S(2)}) collective-permute-start(f32[1,4,128,128]{3,2,1,0:T(8,128)S(1)} %fusion.21), channel_id=1, source_target_pairs={{0,1},{1,2},{2,3},{3,4},{4,5},{5,6},{6,7},{7,8},{8,9},{9,10},{10,1... | collective-permute-start | bytes 786440 | tf_op jit(solution)/shard_map/while/body/eval_jaxpr/ppermute | solution.py:11
  162.0 11.6 %collective-permute-start = (f32[1,4,128,128]{3,2,1,0:T(8,128)S(1)}, f32[1,4,128,128]{3,2,1,0:T(8,128)S(1)}, u32[]{:S(2)}, u32[]{:S(2)}) collective-permute-start(f32[1,4,128,128]{3,2,1,0:T(8,128)S(1)} %fusion.21), channel_id=1, source_target_pairs={{0,1},{1,2},{2,3},{3,4},{4,5},{5,6},{6,7},{7,8},{8,9},{9,10},{10,1... | collective-permute-start | bytes 786440 | tf_op jit(solution)/shard_map/while/body/eval_jaxpr/ppermute | solution.py:11
  173.7 11.6 %collective-permute-start = (f32[1,4,128,128]{3,2,1,0:T(8,128)S(1)}, f32[1,4,128,128]{3,2,1,0:T(8,128)S(1)}, u32[]{:S(2)}, u32[]{:S(2)}) collective-permute-start(f32[1,4,128,128]{3,2,1,0:T(8,128)S(1)} %fusion.21), channel_id=1, source_target_pairs={{0,1},{1,2},{2,3},{3,4},{4,5},{5,6},{6,7},{7,8},{8,9},{9,10},{10,1... | collective-permute-start | bytes 786440 | tf_op jit(solution)/shard_map/while/body/eval_jaxpr/ppermute | solution.py:11
  185.4 11.6 %collective-permute-start = (f32[1,4,128,128]{3,2,1,0:T(8,128)S(1)}, f32[1,4,128,128]{3,2,1,0:T(8,128)S(1)}, u32[]{:S(2)}, u32[]{:S(2)}) collective-permute-start(f32[1,4,128,128]{3,2,1,0:T(8,128)S(1)} %fusion.21), channel_id=1, source_target_pairs={{0,1},{1,2},{2,3},{3,4},{4,5},{5,6},{6,7},{7,8},{8,9},{9,10},{10,1... | collective-permute-start | bytes 786440 | tf_op jit(solution)/shard_map/while/body/eval_jaxpr/ppermute | solution.py:11
  197.2 11.6 %collective-permute-start = (f32[1,4,128,128]{3,2,1,0:T(8,128)S(1)}, f32[1,4,128,128]{3,2,1,0:T(8,128)S(1)}, u32[]{:S(2)}, u32[]{:S(2)}) collective-permute-start(f32[1,4,128,128]{3,2,1,0:T(8,128)S(1)} %fusion.21), channel_id=1, source_target_pairs={{0,1},{1,2},{2,3},{3,4},{4,5},{5,6},{6,7},{7,8},{8,9},{9,10},{10,1... | collective-permute-start | bytes 786440 | tf_op jit(solution)/shard_map/while/body/eval_jaxpr/ppermute | solution.py:11
  208.9 11.6 %collective-permute-start = (f32[1,4,128,128]{3,2,1,0:T(8,128)S(1)}, f32[1,4,128,128]{3,2,1,0:T(8,128)S(1)}, u32[]{:S(2)}, u32[]{:S(2)}) collective-permute-start(f32[1,4,128,128]{3,2,1,0:T(8,128)S(1)} %fusion.21), channel_id=1, source_target_pairs={{0,1},{1,2},{2,3},{3,4},{4,5},{5,6},{6,7},{7,8},{8,9},{9,10},{10,1... | collective-permute-start | bytes 786440 | tf_op jit(solution)/shard_map/while/body/eval_jaxpr/ppermute | solution.py:11
  220.7 11.6 %collective-permute-start = (f32[1,4,128,128]{3,2,1,0:T(8,128)S(1)}, f32[1,4,128,128]{3,2,1,0:T(8,128)S(1)}, u32[]{:S(2)}, u32[]{:S(2)}) collective-permute-start(f32[1,4,128,128]{3,2,1,0:T(8,128)S(1)} %fusion.21), channel_id=1, source_target_pairs={{0,1},{1,2},{2,3},{3,4},{4,5},{5,6},{6,7},{7,8},{8,9},{9,10},{10,1... | collective-permute-start | bytes 786440 | tf_op jit(solution)/shard_map/while/body/eval_jaxpr/ppermute | solution.py:11
  232.4 11.6 %collective-permute-start = (f32[1,4,128,128]{3,2,1,0:T(8,128)S(1)}, f32[1,4,128,128]{3,2,1,0:T(8,128)S(1)}, u32[]{:S(2)}, u32[]{:S(2)}) collective-permute-start(f32[1,4,128,128]{3,2,1,0:T(8,128)S(1)} %fusion.21), channel_id=1, source_target_pairs={{0,1},{1,2},{2,3},{3,4},{4,5},{5,6},{6,7},{7,8},{8,9},{9,10},{10,1... | collective-permute-start | bytes 786440 | tf_op jit(solution)/shard_map/while/body/eval_jaxpr/ppermute | solution.py:11
  244.1 11.6 %collective-permute-start = (f32[1,4,128,128]{3,2,1,0:T(8,128)S(1)}, f32[1,4,128,128]{3,2,1,0:T(8,128)S(1)}, u32[]{:S(2)}, u32[]{:S(2)}) collective-permute-start(f32[1,4,128,128]{3,2,1,0:T(8,128)S(1)} %fusion.21), channel_id=1, source_target_pairs={{0,1},{1,2},{2,3},{3,4},{4,5},{5,6},{6,7},{7,8},{8,9},{9,10},{10,1... | collective-permute-start | bytes 786440 | tf_op jit(solution)/shard_map/while/body/eval_jaxpr/ppermute | solution.py:11
  255.9 11.6 %collective-permute-start = (f32[1,4,128,128]{3,2,1,0:T(8,128)S(1)}, f32[1,4,128,128]{3,2,1,0:T(8,128)S(1)}, u32[]{:S(2)}, u32[]{:S(2)}) collective-permute-start(f32[1,4,128,128]{3,2,1,0:T(8,128)S(1)} %fusion.21), channel_id=1, source_target_pairs={{0,1},{1,2},{2,3},{3,4},{4,5},{5,6},{6,7},{7,8},{8,9},{9,10},{10,1... | collective-permute-start | bytes 786440 | tf_op jit(solution)/shard_map/while/body/eval_jaxpr/ppermute | solution.py:11
  267.6 11.6 %collective-permute-start = (f32[1,4,128,128]{3,2,1,0:T(8,128)S(1)}, f32[1,4,128,128]{3,2,1,0:T(8,128)S(1)}, u32[]{:S(2)}, u32[]{:S(2)}) collective-permute-start(f32[1,4,128,128]{3,2,1,0:T(8,128)S(1)} %fusion.21), channel_id=1, source_target_pairs={{0,1},{1,2},{2,3},{3,4},{4,5},{5,6},{6,7},{7,8},{8,9},{9,10},{10,1... | collective-permute-start | bytes 786440 | tf_op jit(solution)/shard_map/while/body/eval_jaxpr/ppermute | solution.py:11
  279.3 11.6 %collective-permute-start = (f32[1,4,128,128]{3,2,1,0:T(8,128)S(1)}, f32[1,4,128,128]{3,2,1,0:T(8,128)S(1)}, u32[]{:S(2)}, u32[]{:S(2)}) collective-permute-start(f32[1,4,128,128]{3,2,1,0:T(8,128)S(1)} %fusion.21), channel_id=1, source_target_pairs={{0,1},{1,2},{2,3},{3,4},{4,5},{5,6},{6,7},{7,8},{8,9},{9,10},{10,1... | collective-permute-start | bytes 786440 | tf_op jit(solution)/shard_map/while/body/eval_jaxpr/ppermute | solution.py:11
  291.1 11.6 %collective-permute-start = (f32[1,4,128,128]{3,2,1,0:T(8,128)S(1)}, f32[1,4,128,128]{3,2,1,0:T(8,128)S(1)}, u32[]{:S(2)}, u32[]{:S(2)}) collective-permute-start(f32[1,4,128,128]{3,2,1,0:T(8,128)S(1)} %fusion.21), channel_id=1, source_target_pairs={{0,1},{1,2},{2,3},{3,4},{4,5},{5,6},{6,7},{7,8},{8,9},{9,10},{10,1... | collective-permute-start | bytes 786440 | tf_op jit(solution)/shard_map/while/body/eval_jaxpr/ppermute | solution.py:11
  302.8 11.6 %collective-permute-start = (f32[1,4,128,128]{3,2,1,0:T(8,128)S(1)}, f32[1,4,128,128]{3,2,1,0:T(8,128)S(1)}, u32[]{:S(2)}, u32[]{:S(2)}) collective-permute-start(f32[1,4,128,128]{3,2,1,0:T(8,128)S(1)} %fusion.21), channel_id=1, source_target_pairs={{0,1},{1,2},{2,3},{3,4},{4,5},{5,6},{6,7},{7,8},{8,9},{9,10},{10,1... | collective-permute-start | bytes 786440 | tf_op jit(solution)/shard_map/while/body/eval_jaxpr/ppermute | solution.py:11
  314.5 11.6 %collective-permute-start = (f32[1,4,128,128]{3,2,1,0:T(8,128)S(1)}, f32[1,4,128,128]{3,2,1,0:T(8,128)S(1)}, u32[]{:S(2)}, u32[]{:S(2)}) collective-permute-start(f32[1,4,128,128]{3,2,1,0:T(8,128)S(1)} %fusion.21), channel_id=1, source_target_pairs={{0,1},{1,2},{2,3},{3,4},{4,5},{5,6},{6,7},{7,8},{8,9},{9,10},{10,1... | collective-permute-start | bytes 786440 | tf_op jit(solution)/shard_map/while/body/eval_jaxpr/ppermute | solution.py:11
  326.3 11.6 %collective-permute-start = (f32[1,4,128,128]{3,2,1,0:T(8,128)S(1)}, f32[1,4,128,128]{3,2,1,0:T(8,128)S(1)}, u32[]{:S(2)}, u32[]{:S(2)}) collective-permute-start(f32[1,4,128,128]{3,2,1,0:T(8,128)S(1)} %fusion.21), channel_id=1, source_target_pairs={{0,1},{1,2},{2,3},{3,4},{4,5},{5,6},{6,7},{7,8},{8,9},{9,10},{10,1... | collective-permute-start | bytes 786440 | tf_op jit(solution)/shard_map/while/body/eval_jaxpr/ppermute | solution.py:11
  338.0 11.6 %collective-permute-start = (f32[1,4,128,128]{3,2,1,0:T(8,128)S(1)}, f32[1,4,128,128]{3,2,1,0:T(8,128)S(1)}, u32[]{:S(2)}, u32[]{:S(2)}) collective-permute-start(f32[1,4,128,128]{3,2,1,0:T(8,128)S(1)} %fusion.21), channel_id=1, source_target_pairs={{0,1},{1,2},{2,3},{3,4},{4,5},{5,6},{6,7},{7,8},{8,9},{9,10},{10,1... | collective-permute-start | bytes 786440 | tf_op jit(solution)/shard_map/while/body/eval_jaxpr/ppermute | solution.py:11
  349.7 11.6 %collective-permute-start = (f32[1,4,128,128]{3,2,1,0:T(8,128)S(1)}, f32[1,4,128,128]{3,2,1,0:T(8,128)S(1)}, u32[]{:S(2)}, u32[]{:S(2)}) collective-permute-start(f32[1,4,128,128]{3,2,1,0:T(8,128)S(1)} %fusion.21), channel_id=1, source_target_pairs={{0,1},{1,2},{2,3},{3,4},{4,5},{5,6},{6,7},{7,8},{8,9},{9,10},{10,1... | collective-permute-start | bytes 786440 | tf_op jit(solution)/shard_map/while/body/eval_jaxpr/ppermute | solution.py:11
  361.5 11.7 %collective-permute-start = (f32[1,4,128,128]{3,2,1,0:T(8,128)S(1)}, f32[1,4,128,128]{3,2,1,0:T(8,128)S(1)}, u32[]{:S(2)}, u32[]{:S(2)}) collective-permute-start(f32[1,4,128,128]{3,2,1,0:T(8,128)S(1)} %fusion.21), channel_id=1, source_target_pairs={{0,1},{1,2},{2,3},{3,4},{4,5},{5,6},{6,7},{7,8},{8,9},{9,10},{10,1... | collective-permute-start | bytes 786440 | tf_op jit(solution)/shard_map/while/body/eval_jaxpr/ppermute | solution.py:11
  387.1 59.1 %copy-start.2 = (f32[512]{0:T(512)S(1)}, f32[512]{0:T(512)}, u32[]{:S(2)}) copy-start(f32[512]{0:T(512)} %param.12) | copy-start | bytes 6148
  (2 other events, 7.3 us)
